TPU v7x, 128 devices: a whole 4x4x4 slice. The times are simulated.
128 devices in a mesh: ctx: 32 (over y, z, core), fsdp: 4 (over x).
Axes of the slice: x: 4, y: 4, z: 4, core: 2. Of those that a mesh axis runs over, the one named last changes fastest.
Arguments:
- gate_in: bfloat16 [16384, 4096], P('ctx', 'fsdp'), may hold values from -6 to 6
- values: bfloat16 [16384, 4096], P('ctx', 'fsdp'), may hold values from -6 to 6
- gate_out: bfloat16 [16384, 4096], P('ctx', 'fsdp'), may hold values from -6 to 6
- bias: float32 [4096], P('fsdp'), may hold values from -4 to 4
- spectrum: bfloat16 [2, 32768, 4096], P(None, ('ctx', 'fsdp')), may hold values from -6 to 6
Outputs:
- gated: bfloat16 [16384, 4096], P('ctx', 'fsdp')
All inputs are finite; a program needn't handle non-finite values.
Results may differ from a plain program's by a relative error of at most 0.0049.
Values may be sent and summed in bfloat16 or wider, within the bound.
No kernel may reach another device: no remote copies, remote signals or barrier semaphores. Data moves between devices by JAX's collectives and lax.ppermute only.
A program may use at most 128 MiB of HBM per device.

v0:
```python
import math
import jax
import jax.numpy as jnp
from jax import lax
from jax.sharding import PartitionSpec as P


def phase_angles(rows_side, cols_side, modulus):
    product = rows_side[:, None] * cols_side[None, :] % modulus
    return product.astype(jnp.float32) * (2.0 * math.pi / modulus)


def contract(matrix, operand):
    return jnp.einsum("kj,sjc->skc", matrix, operand, precision=lax.Precision.HIGHEST)


def mix_rows(matrix, operand):
    return jnp.einsum("kp,pjc->kjc", matrix, operand, precision=lax.Precision.HIGHEST)


def body(gate_in, values, gate_out, bias, spectrum):
    devices = lax.axis_size("ctx")
    rows_here = gate_in.shape[0]
    channels = gate_in.shape[1]
    block_rows = rows_here // devices
    length_total = 2 * rows_here * devices
    position = lax.axis_index("ctx")
    mixed = (gate_in.astype(jnp.float32) * values.astype(jnp.float32)).astype(jnp.bfloat16)
    mixed = lax.optimization_barrier(mixed)
    member = lax.axis_index("fsdp")
    filter_here = lax.dynamic_slice_in_dim(
        lax.all_gather(spectrum, "fsdp", axis=1, tiled=True), member * channels, channels, 2
    )
    source_index = jnp.arange(devices, dtype=jnp.int32)
    mirror_index = jnp.where(source_index == 0, devices, 2 * devices - source_index)
    radix_order = jnp.stack([source_index, mirror_index], axis=1).reshape(2 * devices)
    cross_angle = phase_angles(radix_order, source_index, 2 * devices)
    cross_cos = jnp.cos(cross_angle)
    cross_sin = jnp.sin(cross_angle)
    local_rows = position * block_rows + jnp.arange(block_rows, dtype=jnp.int32)
    twist_angle = (radix_order[:, None] * local_rows[None, :] % length_total).astype(
        jnp.float32
    ) * (2.0 * math.pi / length_total)
    twist_cos = jnp.cos(twist_angle)[:, :, None]
    twist_sin = jnp.sin(twist_angle)[:, :, None]
    source = mixed[None]
    width_now = source.shape[2]
    real_in = lax.all_to_all(
        source.reshape(source.shape[0], devices, block_rows, width_now),
        "ctx",
        split_axis=1,
        concat_axis=1,
        tiled=True,
    )[0].astype(jnp.float32)
    real_mix = mix_rows(cross_cos, real_in)
    imag_mix = -mix_rows(cross_sin, real_in)
    spread = jnp.stack(
        [real_mix * twist_cos + imag_mix * twist_sin, imag_mix * twist_cos - real_mix * twist_sin]
    )
    regrouped = lax.all_to_all(spread, "ctx", split_axis=1, concat_axis=2, tiled=True)
    row_index = jnp.arange(rows_here, dtype=jnp.int32)
    local_angle = phase_angles(row_index, row_index, rows_here)
    local_cos = jnp.cos(local_angle)
    local_sin = jnp.sin(local_angle)
    real_part = regrouped[0]
    imag_part = regrouped[1]
    freq_real = contract(local_cos, real_part) + contract(local_sin, imag_part)
    freq_imag = contract(local_cos, imag_part) - contract(local_sin, real_part)
    filter_float = filter_here.astype(jnp.float32).reshape(2, 2, rows_here, channels)
    prod_real = freq_real * filter_float[0] - freq_imag * filter_float[1]
    prod_imag = freq_real * filter_float[1] + freq_imag * filter_float[0]
    back_real = contract(local_cos, prod_real) - contract(local_sin, prod_imag)
    back_imag = contract(local_cos, prod_imag) + contract(local_sin, prod_real)
    pair_index = jnp.stack([position, jnp.where(position == 0, devices, 2 * devices - position)])
    back_angle = (pair_index[:, None] * row_index[None, :] % length_total).astype(jnp.float32) * (
        2.0 * math.pi / length_total
    )
    back_cos = jnp.cos(back_angle)[:, :, None]
    back_sin = jnp.sin(back_angle)[:, :, None]
    turned_real = back_real * back_cos - back_imag * back_sin
    turned_imag = back_real * back_sin + back_imag * back_cos
    stacked = jnp.stack([turned_real, turned_imag]).reshape(2, 2, devices, block_rows, width_now)
    inverse_angle = phase_angles(source_index, radix_order, 2 * devices)
    inverse_cos = jnp.cos(inverse_angle) / length_total
    inverse_sin = jnp.sin(inverse_angle) / length_total
    received = lax.all_to_all(stacked, "ctx", split_axis=2, concat_axis=1, tiled=True)
    real_block = received[0, :, 0]
    imag_block = received[1, :, 0]
    real_out = mix_rows(inverse_cos, real_block) - mix_rows(inverse_sin, imag_block)
    folded = real_out[None]
    restored = lax.all_to_all(folded, "ctx", split_axis=1, concat_axis=1, tiled=True)
    restored = restored.reshape(restored.shape[0], rows_here, width_now)
    convolved_part = restored[0]
    convolved = convolved_part + bias[None, :] * mixed.astype(jnp.float32)
    return (gate_out.astype(jnp.float32) * convolved).astype(jnp.bfloat16)


def solution(mesh):
    return jax.shard_map(
        body,
        mesh=mesh,
        in_specs=(
            P("ctx", "fsdp"),
            P("ctx", "fsdp"),
            P("ctx", "fsdp"),
            P("fsdp"),
            P(None, ("ctx", "fsdp"), None),
        ),
        out_specs=P("ctx", "fsdp"),
        check_vma=False,
    )
```

profile of v0, /device:TPU:1, one launch (start us, length us, event | category | flops | bytes accessed | tf_op | source)
XLA Modules:
  0.0 493.6 jit_solution(11693524858831694724)
XLA Ops:
  6.5 0.0 all-gather.2.cloned.1.call-start
  6.5 0.7 all-gather.2.cloned.1.call-update
  7.3 0.5 copy-done.1
  7.8 0.3 copy-done.2
  8.1 1.4 multiply_convert_fusion
  9.4 9.6 %all-to-all-start = ((bf16[1,32,16,1024]{3,2,0,1:T(8,128)(2,1)}), bf16[1,32,16,1024]{3,2,0,1:T(8,128)(2,1)S(1)}, u32[]{:S(2)}, u32[]{:S(2)}) async-start(bf16[1,32,16,1024]{3,2,0,1:T(8,128)(2,1)} %bitcast.3), calls=%async_computation | async-start | bytes 2097152 | tf_op jit(solution)/shard_map/all_to_all | solution.py:48
  19.1 0.1 copy.52
  19.2 0.1 mul.274
  19.3 0.1 fusion.79
  19.4 16.5 %all-to-all-done = bf16[1,32,16,1024]{3,2,0,1:T(8,128)(2,1)S(1)} async-done(((bf16[1,32,16,1024]{3,2,0,1:T(8,128)(2,1)}), bf16[1,32,16,1024]{3,2,0,1:T(8,128)(2,1)S(1)}, u32[]{:S(2)}, u32[]{:S(2)}) %all-to-all-start) | async-done | bytes 1048608 | tf_op jit(solution)/shard_map/all_to_all | solution.py:48
  36.0 2.7 fusion.25
  38.6 3.6 add_bitcast_fusion
  42.2 1.7 pad_maximum_fusion
  43.9 8.3 %copy.55 = f32[2,64,16,1024]{3,2,0,1:T(8,128)} copy(f32[2,64,16,1024]{3,1,2,0:T(8,128)S(1)} %pad_maximum_fusion) | data formatting | bytes 16777216 | tf_op jit(solution)/shard_map/stack | solution.py:57
  52.1 4.8 all-to-all-start.1
  56.9 0.1 pad_add_fusion.1
  57.0 0.2 fusion.81
  57.2 104.1 %all-to-all-done.1 = f32[2,64,16,1024]{3,2,0,1:T(8,128)} async-done(((f32[2,64,16,1024]{3,2,0,1:T(8,128)}), f32[2,64,16,1024]{3,2,0,1:T(8,128)}, u32[]{:S(2)}, u32[]{:S(2)}) %all-to-all-start.1) | async-done | bytes 8388640 | tf_op jit(solution)/shard_map/all_to_all | solution.py:60
  161.3 4.2 copy.56
  165.5 1.7 fusion.134
  167.1 0.5 copy.57
  167.7 0.0 copy-start
  167.7 0.5 copy.59
  168.2 1.4 copy-done
  169.7 17.0 %fusion.23 = f32[2,1024,512]{2,1,0:T(8,128)S(1)} fusion(f32[2,512,1024]{2,1,0:T(8,128)S(1)} %bitcast.102), kind=kOutput, calls=%fused_computation.42 | convolution fusion | flops 6446120960 | bytes 8388608 | tf_op jit(solution)/shard_map/kj,sjc->skc/dot_general | solution.py:14
  186.7 18.7 %fusion.21 = f32[2,1024,512]{2,1,0:T(8,128)} fusion(f32[2,512,1024]{2,1,0:T(8,128)S(1)} %bitcast.100), kind=kOutput, calls=%fused_computation.40 | convolution fusion | flops 6446120960 | bytes 8388608 | tf_op jit(solution)/shard_map/kj,sjc->skc/dot_general | solution.py:14
  205.4 18.5 %convolution_add_fusion.1 = f32[2,1024,512]{2,1,0:T(8,128)} fusion(f32[2,1024,512]{2,1,0:T(8,128)S(1)} %fusion.23, f32[2,512,1024]{2,1,0:T(8,128)S(1)} %bitcast.101), kind=kOutput, calls=%fused_computation.20 | convolution fusion | flops 6447169536 | bytes 12582912 | tf_op jit(solution)/shard_map/kj,sjc->skc/dot_general | solution.py:14
  223.9 3.2 dynamic-slice_convert_fusion
  227.1 4.1 fusion.133
  231.2 5.4 %copy.64 = f32[2,512,1024]{1,2,0:T(8,128)} copy(f32[2,512,1024]{2,1,0:T(8,128)} %bitcast.108) | data formatting | bytes 8388608 | tf_op jit(solution)/shard_map/squeeze | solution.py:70
  236.6 5.4 %copy.61 = f32[2,512,1024]{1,2,0:T(8,128)} copy(f32[2,512,1024]{2,1,0:T(8,128)} %bitcast.107) | data formatting | bytes 8388608 | tf_op jit(solution)/shard_map/squeeze | solution.py:70
  242.1 26.0 %fusion.4 = (f32[2,512,1024]{1,2,0:T(8,128)S(1)}, f32[2,512,1024]{1,2,0:T(8,128)S(1)}) fusion(f32[2,512,1024]{1,2,0:T(8,128)} %copy.64, f32[2,512,1024]{1,2,0:T(8,128)} %copy.61, f32[2,1024,512]{2,1,0:T(8,128)} %convolution_add_fusion.1, f32[2,1024,512]{2,1,0:T(8,128)} %fusion.21, f32[2,512,1024]{2,1,0:T(8,128)} %bitcast.103), kind=kOutput, calls=%fused_computation.8 | convolution fusion | flops 6453460992 | bytes 29360128 | tf_op jit(solution)/shard_map/kj,sjc->skc/dot_general | solution.py:14
  268.0 10.7 %fusion.19 = f32[2,1024,512]{1,2,0:T(8,128)S(1)} fusion(f32[2,512,1024]{1,2,0:T(8,128)S(1)} %get-tuple-element.5), kind=kOutput, calls=%fused_computation.38 | convolution fusion | flops 6446120960 | bytes 8388608 | tf_op jit(solution)/shard_map/kj,sjc->skc/dot_general | solution.py:14
  278.7 11.1 %fusion.17 = f32[2,1024,512]{1,2,0:T(8,128)S(1)} fusion(f32[2,512,1024]{1,2,0:T(8,128)S(1)} %get-tuple-element.6), kind=kOutput, calls=%fused_computation.36 | convolution fusion | flops 6446120960 | bytes 8388608 | tf_op jit(solution)/shard_map/kj,sjc->skc/dot_general | solution.py:14
  289.8 11.2 %convolution_subtract_fusion = f32[2,1024,512]{1,2,0:T(8,128)S(1)} fusion(f32[2,1024,512]{1,2,0:T(8,128)S(1)} %fusion.19, f32[2,512,1024]{1,2,0:T(8,128)S(1)} %get-tuple-element.6), kind=kOutput, calls=%fused_computation.18 | convolution fusion | flops 6447169536 | bytes 12582912 | tf_op jit(solution)/shard_map/kj,sjc->skc/dot_general | solution.py:14
  301.0 12.2 %multiply_subtract_fusion = (f32[2,1024,512]{1,2,0:T(8,128)S(1)}, f32[2,1024,512]{1,2,0:T(8,128)S(1)}) fusion(f32[2,1024,512]{1,2,0:T(8,128)S(1)} %convolution_subtract_fusion, f32[2,512]{1,0:T(2,128)S(1)} %get-tuple-element.20, f32[2,512]{1,0:T(2,128)S(1)} %get-tuple-element.19, f32[2,1024,512]{1,2,0:T(8,128)S(1)} %fusion.17, ...), kind=kOutput, calls=%fused_computation.13 | convolution fusion | flops 6453460992 | bytes 20979712 | tf_op jit(solution)/shard_map/kj,sjc->skc/dot_general | solution.py:14
  313.2 1.7 pad_maximum_fusion.1
  314.9 1.7 copy.84
  316.6 123.0 %all_to_all.40 = f32[2,2,32,16,1024]{4,3,1,0,2:T(8,128)S(1)} all-to-all(f32[2,2,32,16,1024]{4,3,1,0,2:T(8,128)S(1)} %copy.84), channel_id=1, replica_groups=mesh['ctx'=32,'fsdp'=4] {'ctx'}, dimensions={2} | all-to-all | bytes 16777216 | tf_op jit(solution)/shard_map/all_to_all | solution.py:86
  439.6 1.7 fusion.132
  441.2 4.6 fusion
  445.9 4.7 subtract_bitcast_fusion.1
  450.6 0.0 copy-start.3
  450.6 0.0 copy-start.4
  450.6 1.2 copy.75
  451.8 31.8 %all_to_all.41 = f32[1,32,16,1024]{3,2,0,1:T(8,128)S(1)} all-to-all(f32[1,32,16,1024]{3,2,0,1:T(8,128)S(1)} %copy.75), channel_id=1, replica_groups=mesh['ctx'=32,'fsdp'=4] {'ctx'}, dimensions={1} | all-to-all | bytes 4194304 | tf_op jit(solution)/shard_map/all_to_all | solution.py:91
  483.7 0.0 copy-done.3
  483.7 2.9 fusion.7
  (8 shorter events, 0.0 us)
Async XLA Ops:
  6.5 1.2 copy-start.1
  6.5 1.5 copy-start.2
  6.5 217.4 %all-gather.2.cloned.1.call-start = ((), (), s32[]{:S(2)}) async-start(), calls=%async_computation.4 | async-start | bytes 20971520 | tf_op jit(solution)/shard_map/all_gather | solution.py:32
  9.4 26.5 %all-to-all-start = ((bf16[1,32,16,1024]{3,2,0,1:T(8,128)(2,1)}), bf16[1,32,16,1024]{3,2,0,1:T(8,128)(2,1)S(1)}, u32[]{:S(2)}, u32[]{:S(2)}) async-start(bf16[1,32,16,1024]{3,2,0,1:T(8,128)(2,1)} %bitcast.3), calls=%async_computation | async-start | bytes 2097152 | tf_op jit(solution)/shard_map/all_to_all | solution.py:48
  52.1 109.1 %all-to-all-start.1 = ((f32[2,64,16,1024]{3,2,0,1:T(8,128)}), f32[2,64,16,1024]{3,2,0,1:T(8,128)}, u32[]{:S(2)}, u32[]{:S(2)}) async-start(f32[2,64,16,1024]{3,2,0,1:T(8,128)} %copy.55), calls=%async_computation.1 | async-start | bytes 16777216 | tf_op jit(solution)/shard_map/all_to_all | solution.py:60
  167.7 2.0 copy-start
  450.6 33.1 %copy-start.3 = (bf16[512,1024]{1,0:T(8,128)(2,1)S(1)}, bf16[512,1024]{1,0:T(8,128)(2,1)}, u32[]{:S(2)}) copy-start(bf16[512,1024]{1,0:T(8,128)(2,1)} %param.7) | copy-start | bytes 3145732
  450.6 33.1 %copy-start.4 = (f32[1024]{0:T(1024)S(1)}, f32[1024]{0:T(1024)}, u32[]{:S(2)}) copy-start(f32[1024]{0:T(1024)} %param.8) | copy-start | bytes 12292
Sparse Core Ops, SparseCore 0:
  9.0 157.0 all-gather.1
where the time goes:
time: 503 us; the launch traced here: 494 us
  blocking collectives  155 us (31%)
  matrix products  141 us (28%)
  waiting for transfers between devices  121 us (24%)
  local copies, waits for them, and re-layouts  37.1 us (7%)
  starting transfers between devices  14.4 us (3%)
  between operations  13.8 us (3%)
  other arithmetic  11.1 us (2%)
    dot_general x8, matrix products, contract(): jnp.einsum('kj,sjc->skc', matrix, operand, precision=lax.Precision.HIGHEST)  125 us
    all_to_all x1, blocking collectives, body(): lax.all_to_all(stacked, 'ctx', split_axis=2, concat_axis=1, tiled=True)  123 us
    all_to_all x1, waiting for transfers between devices, body(): lax.all_to_all(spread, 'ctx', split_axis=1, concat_axis=2, tiled=True)  104 us
    all_to_all x1, blocking collectives, body(): lax.all_to_all(folded, 'ctx', split_axis=1, concat_axis=1, tiled=True)  31.8 us
    all_to_all x1, waiting for transfers between devices, body(): lax.all_to_all(source.reshape(source.shape[0], devices, block_rows, width...  16.5 us
    dot_general x4, matrix products, mix_rows(): jnp.einsum('kp,pjc->kjc', matrix, operand, precision=lax.Precision.HIGHEST)  15.6 us
    squeeze x2, local copies, waits for them, and re-layouts, body(): prod_real = freq_real * filter_float[0] - freq_imag * filter_float[1]  10.8 us
  transfers between devices with their start and end apart: 3, of which 2 were waited for; matrix products, arithmetic and copies ran while one was open for 16% of the time, Pallas kernels for 0%

commit v1 on v0

--- a/solution.py
+++ b/solution.py
@@ -45,12 +45,20 @@
     twist_sin = jnp.sin(twist_angle)[:, :, None]
     source = mixed[None]
     width_now = source.shape[2]
-    real_in = lax.all_to_all(
-        source.reshape(source.shape[0], devices, block_rows, width_now),
-        "ctx",
-        split_axis=1,
-        concat_axis=1,
-        tiled=True,
+    real_in = jnp.concatenate(
+        lax.all_to_all(
+            jnp.stack(
+                jnp.split(
+                    source.reshape(source.shape[0], devices, block_rows, width_now),
+                    lax.axis_size("ctx"),
+                    axis=1,
+                )
+            ),
+            "ctx",
+            0,
+            0,
+        ),
+        axis=1,
     )[0].astype(jnp.float32)
     real_mix = mix_rows(cross_cos, real_in)
     imag_mix = -mix_rows(cross_sin, real_in)

time: 503 us -> 576 us (1.15)
  local copies, waits for them, and re-layouts: 37.1 us -> 109 us
    unnamed x10 -> x41, local copies, waits for them, and re-layouts: 2.27 us -> 19.6 us
    squeeze x0 -> x2, local copies, waits for them, and re-layouts: none -> 12.3 us  [the longest x1 6.22 us: body(): imag_block = received[1, :, 0]]
    slice x2, local copies, waits for them, and re-layouts: 2.18 us -> 13.7 us  [body(): real_part = regrouped[0]]
    all_to_all x1, local copies, waits for them, and re-layouts: 4.23 us -> 15.4 us  [body(): lax.all_to_all(spread, 'ctx', split_axis=1, concat_axis=2, tiled=True)]
    slice x0 -> x2, local copies, waits for them, and re-layouts: none -> 8.42 us  [body(): imag_block = received[1, :, 0]]
  transfers between devices with their start and end apart: 3 -> 3, of which waited for: 2 -> 2; matrix products, arithmetic and copies ran while one was open for 16% -> 22% of each run, Pallas kernels for 0% -> 0%
where the time goes in v1:
time: 576 us; the launch traced here: 566 us
  blocking collectives  155 us (27%)
  matrix products  142 us (25%)
  waiting for transfers between devices  121 us (21%)
  local copies, waits for them, and re-layouts  109 us (19%)
  starting transfers between devices  14.3 us (2%)
  between operations  13.8 us (2%)
  other arithmetic  10.1 us (2%)
    dot_general x8, matrix products, contract(): jnp.einsum('kj,sjc->skc', matrix, operand, precision=lax.Precision.HIGHEST)  125 us
    all_to_all x1, blocking collectives, body(): lax.all_to_all(stacked, 'ctx', split_axis=2, concat_axis=1, tiled=True)  123 us
    all_to_all x1, waiting for transfers between devices, body(): lax.all_to_all(spread, 'ctx', split_axis=1, concat_axis=2, tiled=True)  104 us
    all_to_all x1, blocking collectives, body(): lax.all_to_all(folded, 'ctx', split_axis=1, concat_axis=1, tiled=True)  31.8 us
    unnamed x41, local copies, waits for them, and re-layouts  19.6 us
    dot_general x4, matrix products, mix_rows(): jnp.einsum('kp,pjc->kjc', matrix, operand, precision=lax.Precision.HIGHEST)  17.3 us
    all_to_all x1, waiting for transfers between devices, body(): lax.all_to_all(jnp.stack(jnp.split(source.reshape(source.shape[0], device...  16.5 us
    all_to_all x1, local copies, waits for them, and re-layouts, body(): lax.all_to_all(spread, 'ctx', split_axis=1, concat_axis=2, tiled=True)  15.4 us
  transfers between devices with their start and end apart: 3, of which 2 were waited for; matrix products, arithmetic and copies ran while one was open for 22% of the time, Pallas kernels for 0%

profile of v1, /device:TPU:1, one launch (start us, length us, event | category | flops | bytes accessed | tf_op | source)
XLA Modules:
  0.0 565.8 jit_solution(1783539589394685823)
XLA Ops:
  6.5 0.7 all-gather.2.cloned.1.call-update
  7.8 1.6 multiply_convert_fusion
  9.4 0.6 constant_dynamic-update-slice_fusion.31
  10.0 0.6 constant_dynamic-update-slice_fusion.30
  10.6 0.6 constant_dynamic-update-slice_fusion.29
  11.2 0.6 constant_dynamic-update-slice_fusion.28
  11.9 0.6 constant_dynamic-update-slice_fusion.27
  15.6 0.6 constant_dynamic-update-slice_fusion.21
  23.0 0.6 constant_dynamic-update-slice_fusion.9
  27.3 0.6 constant_dynamic-update-slice_fusion.2
  29.1 9.6 %all-to-all-start = ((bf16[32,1,1,16,1024]{4,3,2,1,0:T(8,128)(2,1)}), bf16[32,1,1,16,1024]{4,3,2,1,0:T(8,128)(2,1)S(1)}, u32[]{:S(2)}, u32[]{:S(2)}) async-start(bf16[32,1,1,16,1024]{4,3,2,1,0:T(8,128)(2,1)} %constant_dynamic-update-slice_fusion), calls=%async_computation | async-start | bytes 2097152 | tf_op jit(solution)/shard_map/all_to_all | solution.py:49
  39.1 16.5 %all-to-all-done = bf16[32,1,1,16,1024]{4,3,2,1,0:T(8,128)(2,1)S(1)} async-done(((bf16[32,1,1,16,1024]{4,3,2,1,0:T(8,128)(2,1)}), bf16[32,1,1,16,1024]{4,3,2,1,0:T(8,128)(2,1)S(1)}, u32[]{:S(2)}, u32[]{:S(2)}) %all-to-all-start) | async-done | bytes 1048608 | tf_op jit(solution)/shard_map/all_to_all | solution.py:49
  55.6 2.7 fusion.19
  58.3 3.6 add_bitcast_fusion
  61.9 1.7 pad_maximum_fusion
  63.6 8.6 %copy.1475 = f32[2,64,16,1024]{3,2,0,1:T(8,128)} copy(f32[2,64,16,1024]{3,1,2,0:T(8,128)S(1)} %pad_maximum_fusion) | data formatting | bytes 16777216 | tf_op jit(solution)/shard_map/stack | solution.py:65
  72.1 4.8 all-to-all-start.1
  77.1 104.1 %all-to-all-done.1 = f32[2,64,16,1024]{3,2,0,1:T(8,128)} async-done(((f32[2,64,16,1024]{3,2,0,1:T(8,128)}), f32[2,64,16,1024]{3,2,0,1:T(8,128)}, u32[]{:S(2)}, u32[]{:S(2)}) %all-to-all-start.1) | async-done | bytes 8388640 | tf_op jit(solution)/shard_map/all_to_all | solution.py:68
  181.2 15.4 %copy.1517 = f32[2,32,2,16,1024]{4,2,1,3,0:T(2,128)} copy(f32[2,32,2,16,1024]{4,3,0,2,1:T(8,128)} %bitcast.39) | data formatting | bytes 16777216 | tf_op jit(solution)/shard_map/all_to_all | solution.py:68
  196.6 9.1 %fusion.129 = (f32[1,2,32,16,1024]{4,1,2,3,0:T(2,128)}, f32[1,2,32,16,1024]{4,1,2,3,0:T(2,128)S(1)}) fusion(f32[2,2,32,16,1024]{4,1,2,3,0:T(2,128)} %bitcast.237), kind=kLoop, calls=%fused_computation.223 | loop fusion | bytes 16777216 | tf_op jit(solution)/shard_map/slice | solution.py:73
  205.8 4.6 copy.1477
  210.4 2.4 copy.1479
  212.8 17.2 %fusion.17 = f32[2,1024,512]{2,1,0:T(8,128)S(1)} fusion(f32[2,512,1024]{2,1,0:T(8,128)S(1)} %bitcast.235), kind=kOutput, calls=%fused_computation.40 | convolution fusion | flops 6446120960 | bytes 8388608 | tf_op jit(solution)/shard_map/kj,sjc->skc/dot_general | solution.py:14
  230.0 18.3 %fusion.15 = f32[2,1024,512]{2,1,0:T(8,128)} fusion(f32[2,512,1024]{2,1,0:T(8,128)S(1)} %bitcast.233), kind=kOutput, calls=%fused_computation.38 | convolution fusion | flops 6446120960 | bytes 8388608 | tf_op jit(solution)/shard_map/kj,sjc->skc/dot_general | solution.py:14
  248.3 18.8 %convolution_add_fusion.1 = f32[2,1024,512]{2,1,0:T(8,128)} fusion(f32[2,1024,512]{2,1,0:T(8,128)S(1)} %fusion.17, f32[2,512,1024]{2,1,0:T(8,128)S(1)} %bitcast.234), kind=kOutput, calls=%fused_computation.18 | convolution fusion | flops 6447169536 | bytes 12582912 | tf_op jit(solution)/shard_map/kj,sjc->skc/dot_general | solution.py:14
  267.1 3.2 dynamic-slice_convert_fusion
  270.3 4.1 fusion.128
  274.4 5.4 copy.1484
  279.8 5.4 copy.1481
  285.2 25.7 %fusion = (f32[2,512,1024]{1,2,0:T(8,128)S(1)}, f32[2,512,1024]{1,2,0:T(8,128)S(1)}) fusion(f32[2,512,1024]{1,2,0:T(8,128)} %copy.1484, f32[2,512,1024]{1,2,0:T(8,128)} %copy.1481, f32[2,1024,512]{2,1,0:T(8,128)} %convolution_add_fusion.1, f32[2,1024,512]{2,1,0:T(8,128)} %fusion.15, f32[2,512,1024]{2,1,0:T(8,128)} %bitcast.236), kind=kOutput, calls=%fused_computation.6 | convolution fusion | flops 6453460992 | bytes 29360128 | tf_op jit(solution)/shard_map/kj,sjc->skc/dot_general | solution.py:14
  311.0 10.7 %fusion.13 = f32[2,1024,512]{1,2,0:T(8,128)S(1)} fusion(f32[2,512,1024]{1,2,0:T(8,128)S(1)} %get-tuple-element.5), kind=kOutput, calls=%fused_computation.36 | convolution fusion | flops 6446120960 | bytes 8388608 | tf_op jit(solution)/shard_map/kj,sjc->skc/dot_general | solution.py:14
  321.6 11.3 %fusion.11 = f32[2,1024,512]{1,2,0:T(8,128)S(1)} fusion(f32[2,512,1024]{1,2,0:T(8,128)S(1)} %get-tuple-element.6), kind=kOutput, calls=%fused_computation.34 | convolution fusion | flops 6446120960 | bytes 8388608 | tf_op jit(solution)/shard_map/kj,sjc->skc/dot_general | solution.py:14
  333.0 11.2 %convolution_subtract_fusion = f32[2,1024,512]{1,2,0:T(8,128)S(1)} fusion(f32[2,1024,512]{1,2,0:T(8,128)S(1)} %fusion.13, f32[2,512,1024]{1,2,0:T(8,128)S(1)} %get-tuple-element.6), kind=kOutput, calls=%fused_computation.16 | convolution fusion | flops 6447169536 | bytes 12582912 | tf_op jit(solution)/shard_map/kj,sjc->skc/dot_general | solution.py:14
  344.2 12.0 %multiply_subtract_fusion = (f32[2,1024,512]{1,2,0:T(8,128)S(1)}, f32[2,1024,512]{1,2,0:T(8,128)S(1)}) fusion(f32[2,1024,512]{1,2,0:T(8,128)S(1)} %convolution_subtract_fusion, f32[2,512]{1,0:T(2,128)S(1)} %get-tuple-element.20, f32[2,512]{1,0:T(2,128)S(1)} %get-tuple-element.19, f32[2,1024,512]{1,2,0:T(8,128)S(1)} %fusion.11, ...), kind=kOutput, calls=%fused_computation.11 | convolution fusion | flops 6453460992 | bytes 20979712 | tf_op jit(solution)/shard_map/kj,sjc->skc/dot_general | solution.py:14
  356.2 1.7 pad_maximum_fusion.1
  357.8 1.7 copy.1491
  359.5 123.4 %all_to_all.40 = f32[2,2,32,16,1024]{4,3,1,0,2:T(8,128)} all-to-all(f32[2,2,32,16,1024]{4,3,1,0,2:T(8,128)S(1)} %copy.1491), channel_id=1, replica_groups=mesh['ctx'=32,'fsdp'=4] {'ctx'}, dimensions={2} | all-to-all | bytes 16777216 | tf_op jit(solution)/shard_map/all_to_all | solution.py:94
  482.9 4.2 copy.1518
  487.1 3.2 fusion.127
  490.3 5.2 copy.1493
  495.5 6.1 %squeeze.24 = f32[64,16,1024]{2,0,1:T(8,128)} reshape(f32[1,32,2,1,16,1024]{5,2,1,4,3,0:T(2,128)} %copy.1493) | data formatting | bytes 8388608 | tf_op jit(solution)/shard_map/squeeze | solution.py:95
  501.6 5.9 %fusion.47 = f32[32,16,1024]{2,0,1:T(8,128)} fusion(f32[64,16,1024]{2,0,1:T(8,128)} %squeeze.24, s32[64]{0:T(128)S(1)} %mul.274), kind=kOutput, calls=%fused_computation.132 | convolution fusion | flops 402683904 | bytes 6291712 | tf_op jit(solution)/shard_map/kp,pjc->kjc/dot_general | solution.py:18
  507.5 5.2 copy.1494
  512.7 6.2 %squeeze.25 = f32[64,16,1024]{2,0,1:T(8,128)} reshape(f32[1,32,2,1,16,1024]{5,2,1,4,3,0:T(2,128)} %copy.1494) | data formatting | bytes 8388608 | tf_op jit(solution)/shard_map/squeeze | solution.py:96
  518.9 5.1 subtract_bitcast_fusion.1
  524.1 1.2 copy.1495
  525.3 31.8 %all_to_all.41 = f32[1,32,16,1024]{3,2,0,1:T(8,128)S(1)} all-to-all(f32[1,32,16,1024]{3,2,0,1:T(8,128)S(1)} %copy.1495), channel_id=1, replica_groups=mesh['ctx'=32,'fsdp'=4] {'ctx'}, dimensions={1} | all-to-all | bytes 4194304 | tf_op jit(solution)/shard_map/all_to_all | solution.py:99
  557.2 1.6 fusion.3
  (45 shorter events, 15.9 us)
Async XLA Ops:
  6.5 1.2 copy-start.2
  6.5 260.6 %all-gather.2.cloned.1.call-start = ((), (), s32[]{:S(2)}) async-start(), calls=%async_computation.4 | async-start | bytes 20971520 | tf_op jit(solution)/shard_map/all_gather | solution.py:32
  29.1 26.5 %all-to-all-start = ((bf16[32,1,1,16,1024]{4,3,2,1,0:T(8,128)(2,1)}), bf16[32,1,1,16,1024]{4,3,2,1,0:T(8,128)(2,1)S(1)}, u32[]{:S(2)}, u32[]{:S(2)}) async-start(bf16[32,1,1,16,1024]{4,3,2,1,0:T(8,128)(2,1)} %constant_dynamic-update-slice_fusion), calls=%async_computation | async-start | bytes 2097152 | tf_op jit(solution)/shard_map/all_to_all | solution.py:49
  72.1 109.1 %all-to-all-start.1 = ((f32[2,64,16,1024]{3,2,0,1:T(8,128)}), f32[2,64,16,1024]{3,2,0,1:T(8,128)}, u32[]{:S(2)}, u32[]{:S(2)}) async-start(f32[2,64,16,1024]{3,2,0,1:T(8,128)} %copy.1475), calls=%async_computation.1 | async-start | bytes 16777216 | tf_op jit(solution)/shard_map/all_to_all | solution.py:68
  210.4 2.4 copy-start
  501.6 5.9 %copy-start.1 = (f32[1,32,2,1,16,1024]{5,4,1,2,0,3:T(8,128)S(1)}, f32[1,32,2,1,16,1024]{5,4,1,2,0,3:T(8,128)}, u32[]{:S(2)}) copy-start(f32[1,32,2,1,16,1024]{5,4,1,2,0,3:T(8,128)} %get-tuple-element.11) | copy-start | bytes 12582916
  524.1 33.1 %copy-start.3 = (bf16[512,1024]{1,0:T(8,128)(2,1)S(1)}, bf16[512,1024]{1,0:T(8,128)(2,1)}, u32[]{:S(2)}) copy-start(bf16[512,1024]{1,0:T(8,128)(2,1)} %param.7) | copy-start | bytes 3145732
  524.1 33.1 %copy-start.4 = (f32[1024]{0:T(1024)S(1)}, f32[1024]{0:T(1024)}, u32[]{:S(2)}) copy-start(f32[1024]{0:T(1024)} %param.8) | copy-start | bytes 12292
Sparse Core Ops, SparseCore 0:
  9.0 157.0 all-gather.1
